TPU v7x, 32 devices: a whole 2x2x4 slice. The times are simulated.
32 devices in a mesh: dp: 2 (over x), context: 16 (over z, y, core).
Axes of the slice: x: 2, y: 2, z: 4, core: 2. Of those that a mesh axis runs over, the one named last changes fastest.
Arguments:
- grad_out: bfloat16 [2, 2048, 4096], P('dp', 'context'), may hold values from -6 to 6
- attn: bfloat16 [2, 2048, 4096], P('dp', 'context'), may hold values from -0.09375 to 0.09375
- w_out: bfloat16 [4096, 4096], P('context'), may hold values from -0.09375 to 0.09375
Outputs:
- grad_attn: bfloat16 [2, 2048, 4096], P('dp', None, 'context')
- grad_w: bfloat16 [4096, 4096], P('context')
All inputs are finite; a program needn't handle non-finite values.
Results may differ from a plain program's by a relative error of at most 0.013.
Values may be sent and summed in bfloat16 or wider, within the bound.
A program may use at most 128 MiB of HBM per device.

v0:
```python
import functools

import jax
import jax.numpy as jnp
from jax import lax
from jax.experimental import pallas as pl
from jax.experimental.pallas import tpu as pltpu
from jax.sharding import PartitionSpec as P

CHUNKS = 16
AHEAD = 2
AHEAD_Y = 8
CORES = 2


def grid_of(chips):
    fast = 1
    while (2 * fast) * (2 * fast) <= chips:
        fast *= 2
    return chips // fast, fast


def kernel(dp, n, chunks, g_in, a_in, w_in, o_attn, o_w, gath, acts, acts_t, w, acc, part, stage_w, stage_a,
           g_send, g_recv, p_send, p_recv, a_send, a_recv, x_send, x_recv, own_sem, w_sem, own_a_sem, ow_sem, oa_sem):
    A, B = grid_of(n // CORES)
    tokens, width = g_in.shape
    heads = w_in.shape[0]
    F = width // chunks
    me = lax.axis_index("context")
    rep = lax.axis_index("dp")
    c = lax.rem(me, CORES)
    b = lax.rem(me // CORES, B)
    a = me // (CORES * B)

    def ctx(a_, b_, c_):
        return (a_ * B + b_) * CORES + c_

    def others(i, size):
        return [lax.rem(i + d, size) for d in range(1, size)]

    def cols(k):
        return pl.ds(pl.multiple_of(k * F, F), F)

    def rows(j):
        return pl.ds(pl.multiple_of(j * tokens, tokens), tokens)

    def block(k, j):
        return gath.at[k, rows(j)]

    def move(src, k, j, target, slot):
        return pltpu.make_async_remote_copy(
            src_ref=src, dst_ref=block(k, j), send_sem=g_send.at[k, slot], recv_sem=g_recv.at[k, j],
            device_id={"context": target}, device_id_type=pl.DeviceIdType.MESH)

    def arrived(k, j):
        move(block(k, j), k, j, me, 0).wait_recv()

    barrier = pltpu.get_barrier_semaphore()
    for j in others(me, n):
        pl.semaphore_signal(barrier, inc=1, device_id={"context": j}, device_id_type=pl.DeviceIdType.MESH)
    for r in others(rep, dp):
        pl.semaphore_signal(barrier, inc=1, device_id={"dp": r}, device_id_type=pl.DeviceIdType.MESH)
    pl.semaphore_wait(barrier, n - 1 + dp - 1)

    Z0, Y0 = 0, A + 1
    S0 = Y0 + A * (B - 1)
    pair = a + 1 - 2 * lax.rem(a, 2)
    side = tokens // 4

    def own(k):
        return g_in.at[:, cols(k)]

    def part_of(k, j, first):
        size = side if first else tokens - side
        lo = pl.multiple_of(j * tokens + (0 if first else side), 16)
        return gath.at[k, pl.ds(lo, size)]

    def inside(t):
        return jnp.logical_and(t >= 0, t < A)

    def z_moves(k, act):
        for sign, slot in ((1, Z0 + a), (-1, Z0 + A)):
            @pl.when(inside(a + sign))
            def _():
                act(move(own(k), k, me, ctx(a + sign, b, c), slot))

    def y_own_moves(k, act):
        for i, t in enumerate(others(b, B)):
            act(move(own(k), k, me, ctx(a, t, c), Y0 + a * (B - 1) + i))

    def sib_own(k, act):
        act(move(own(k), k, me, ctx(a, b, 1 - c), S0 + a))

    def rest_move(k, j, target, slot):
        return pltpu.make_async_remote_copy(
            src_ref=part_of(k, j, False), dst_ref=part_of(k, j, False), send_sem=g_send.at[k, slot],
            recv_sem=g_recv.at[k, j], device_id={"context": target}, device_id_type=pl.DeviceIdType.MESH)

    def side_move(k, j, target, i):
        return pltpu.make_async_remote_copy(
            src_ref=part_of(k, j, True), dst_ref=part_of(k, j, True), send_sem=p_send.at[k, i],
            recv_sem=p_recv.at[k, j], device_id={"context": target}, device_id_type=pl.DeviceIdType.MESH)

    def side_moves(k, act, wait):
        for i, u in enumerate(others(b, B)):
            j = ctx(a, u, c)
            if wait:
                arrived(k, j)
            act(side_move(k, j, ctx(pair, b, c), i))
            act(move(block(k, j), k, j, ctx(a, b, 1 - c), S0 + A * (1 + i) + a))

    def column_moves(k, d, act, wait):
        for sign in (1, -1):
            t = a + sign * d

            @pl.when(inside(t))
            def _():
                j = ctx(t, b, c)
                if wait:
                    arrived(k, j)

                @pl.when(inside(a - sign))
                def _():
                    act(move(block(k, j), k, j, ctx(a - sign, b, c), Z0 + t))
                for i, u in enumerate(others(b, B)):
                    slot = Y0 + t * (B - 1) + i
                    if d > 1:
                        act(move(block(k, j), k, j, ctx(a, u, c), slot))
                    else:
                        @pl.when(t == pair)
                        def _():
                            act(rest_move(k, j, ctx(a, u, c), slot))

                        @pl.when(t != pair)
                        def _():
                            act(move(block(k, j), k, j, ctx(a, u, c), slot))
                act(move(block(k, j), k, j, ctx(a, b, 1 - c), S0 + t))

    def plane_moves(k, act, wait):
        for i, u in enumerate(others(b, B)):
            for d in range(1, A):
                t = lax.rem(a + d, A)
                j = ctx(t, u, c)
                if wait:
                    @pl.when(t == pair)
                    def _():
                        rest_move(k, j, me, 0).wait_recv()
                        side_move(k, j, me, 0).wait_recv()

                    @pl.when(t != pair)
                    def _():
                        arrived(k, j)
                act(move(block(k, j), k, j, ctx(a, b, 1 - c), S0 + A * (1 + i) + t))

    def own_copy(k):
        return pltpu.make_async_copy(own(k), block(k, me), own_sem.at[k])

    def w_copy(k):
        return pltpu.make_async_copy(w_in.at[:, cols(k)], w.at[k], w_sem.at[k])

    def head_cols(j):
        return pl.ds(pl.multiple_of(j * heads, heads), heads)

    def act_move(i, target):
        return pltpu.make_async_remote_copy(
            src_ref=a_in.at[:, head_cols(target)], dst_ref=acts.at[me], send_sem=a_send.at[i],
            recv_sem=a_recv.at[me], device_id={"context": target}, device_id_type=pl.DeviceIdType.MESH)

    own_act = pltpu.make_async_copy(a_in.at[:, head_cols(me)], acts.at[me], own_a_sem)

    def start(m):
        m.start()

    def done(m):
        m.wait_send()

    def x_moves(k, act):
        for i, r in enumerate(others(rep, dp)):
            act(pltpu.make_async_remote_copy(
                src_ref=part.at[rep, k], dst_ref=part.at[rep, k], send_sem=x_send.at[k, i],
                recv_sem=x_recv.at[k, rep], device_id={"dp": r}, device_id_type=pl.DeviceIdType.MESH))

    def x_arrived(k):
        for r in others(rep, dp):
            pltpu.make_async_remote_copy(
                src_ref=part.at[r, k], dst_ref=part.at[r, k], send_sem=x_send.at[k, 0],
                recv_sem=x_recv.at[k, r], device_id={"dp": rep}, device_id_type=pl.DeviceIdType.MESH).wait_recv()

    for k in range(AHEAD):
        z_moves(k, start)
    targets = others(me, n)
    for i, t in enumerate(targets):
        act_move(i, t).start()
    own_act.start()

    for k in range(AHEAD_Y):
        y_own_moves(k, start)
        sib_own(k, start)

    @pl.loop(0, chunks)
    def _(k):
        own_copy(k).start()
        w_copy(k).start()

    row_tile = min(512, tokens * n)
    tiles = tokens * n // row_tile

    def out_attn(i):
        r = pl.ds(pl.multiple_of(i * row_tile, row_tile), row_tile)
        return pltpu.make_async_copy(stage_a.at[r], o_attn.at[r], oa_sem.at[i])

    def compute(k):
        own_copy(k).wait()
        w_copy(k).wait()
        for t in range(A):
            for u in range(B):
                arrived(k, ctx(t, u, 1 - c))

        @pl.when(k == 0)
        def _():
            own_act.wait()
            for t in targets:
                pltpu.make_async_remote_copy(
                    src_ref=acts.at[t], dst_ref=acts.at[t], send_sem=a_send.at[0], recv_sem=a_recv.at[t],
                    device_id={"context": me}, device_id_type=pl.DeviceIdType.MESH).wait_recv()
            for j in range(n):
                acts_t[:, j * tokens:(j + 1) * tokens] = acts[j].T
            acc[...] = jnp.zeros_like(acc)

        part[rep, k] = jnp.dot(acts_t[...], gath[k], preferred_element_type=jnp.float32).astype(part.dtype)
        x_moves(k, start)

        @pl.loop(0, tiles)
        def _(i):
            r = pl.ds(pl.multiple_of(i * row_tile, row_tile), row_tile)
            total = acc[r] + lax.dot_general(
                gath[k, r], w[k], (((1,), (1,)), ((), ())), preferred_element_type=jnp.float32)

            @pl.when(k < chunks - 1)
            def _():
                acc[r] = total

            @pl.when(k == chunks - 1)
            def _():
                stage_a[r] = total.astype(stage_a.dtype)
                out_attn(i).start()

    def out_w(k):
        return pltpu.make_async_copy(stage_w.at[k], o_w.at[:, cols(k)], ow_sem.at[k])

    def finish(k):
        x_arrived(k)
        total = part[0, k].astype(jnp.float32)
        for r in range(1, dp):
            total += part[r, k].astype(jnp.float32)
        stage_w[k] = total.astype(stage_w.dtype)
        out_w(k).start()

    def stage(k, f):
        pl.when(jnp.logical_and(k >= 0, k < chunks))(functools.partial(f, k))

    @pl.loop(0, chunks + A + 2)
    def _(i):
        def ahead_z(k):
            z_moves(k, start)

        def ahead_y(k):
            y_own_moves(k, start)
            sib_own(k, start)

        stage(i + AHEAD, ahead_z)
        stage(i + AHEAD_Y, ahead_y)
        for d in range(1, A):
            stage(i - d + 1, lambda k, d=d: column_moves(k, d, start, True))
            if d == 1:
                stage(i, lambda k: side_moves(k, start, True))
        stage(i - A + 1, lambda k: plane_moves(k, start, True))
        stage(i - A, compute)
        stage(i - A - 1, finish)

    @pl.loop(0, chunks)
    def _(k):
        z_moves(k, done)
        y_own_moves(k, done)
        sib_own(k, done)
        side_moves(k, done, False)
        for d in range(1, A):
            column_moves(k, d, done, False)
        plane_moves(k, done, False)
        x_moves(k, done)
        out_w(k).wait()

    for i, t in enumerate(targets):
        act_move(i, t).wait_send()

    @pl.loop(0, tiles)
    def _(i):
        out_attn(i).wait()


def local(dp, n, grad_out, attn, w_out):
    g, x = grad_out[0], attn[0]
    tokens, width = g.shape
    heads = w_out.shape[0]
    length = tokens * n
    chunks = CHUNKS
    F = width // chunks
    A, B = grid_of(n // CORES)
    sends = A + 1 + A * (B - 1) + A * B
    tiles = length // min(512, length)
    any_ = pl.BlockSpec(memory_space=pl.ANY)
    bf = jnp.bfloat16
    dma = pltpu.SemaphoreType.DMA
    h, gw = pl.pallas_call(
        functools.partial(kernel, dp, n, chunks),
        out_shape=(jax.ShapeDtypeStruct((length, heads), bf), jax.ShapeDtypeStruct((heads, width), bf)),
        in_specs=[any_] * 3,
        out_specs=(any_, any_),
        scratch_shapes=[
            pltpu.VMEM((chunks, length, F), bf),
            pltpu.VMEM((n, tokens, heads), bf),
            pltpu.VMEM((heads, length), bf),
            pltpu.VMEM((chunks, heads, F), bf),
            pltpu.VMEM((length, heads), jnp.float32),
            pltpu.VMEM((dp, chunks, heads, F), bf),
            pltpu.VMEM((chunks, heads, F), bf),
            pltpu.VMEM((length, heads), bf),
            dma((chunks, sends)), dma((chunks, n)), dma((chunks, B - 1)), dma((chunks, n)),
            dma((n - 1,)), dma((n,)),
            dma((chunks, dp - 1)), dma((chunks, dp)),
            dma((chunks,)), dma((chunks,)), dma, dma((chunks,)), dma((tiles,)),
        ],
        compiler_params=pltpu.CompilerParams(
            collective_id=0, has_side_effects=True, vmem_limit_bytes=52 * 2**20),
    )(g, x, w_out)
    return h[None], gw


def solution(mesh):
    dp, n = mesh.shape["dp"], mesh.shape["context"]
    in_specs = (P("dp", "context", None), P("dp", "context", None), P("context", None))
    out_specs = (P("dp", None, "context"), P("context", None))
    return jax.shard_map(functools.partial(local, dp, n), mesh=mesh, in_specs=in_specs, out_specs=out_specs,
                         check_vma=False)
```

profile of v0, /device:TPU:0, one launch (start us, length us, event | category | flops | bytes accessed | tf_op | source)
XLA Modules:
  0.0 128.8 jit_solution(7515429874484122125)
XLA Ops:
  0.6 124.9 %shard_map.50 = (bf16[2048,256]{1,0:T(8,128)(2,1)S(1)}, bf16[256,4096]{1,0:T(8,128)(2,1)}) custom-call(bf16[128,4096]{1,0:T(8,128)(2,1)} %bitcast.4, bf16[128,4096]{1,0:T(8,128)(2,1)} %bitcast.5, bf16[256,4096]{1,0:T(8,128)(2,1)} %w_in.1), custom_call_target="tpu_custom_call" | custom-call | tf_op jit(solution)/shard_map/pallas_call | solution.py:314
  125.5 0.0 copy-start
  125.5 1.0 copy.7
  126.5 1.0 copy-done
  127.5 1.3 %copy.8 = bf16[256,4096]{1,0:T(8,128)(2,1)} copy(bf16[256,4096]{1,0:T(8,128)(2,1)S(1)} %copy-done) | data formatting | bytes 4194304
Async XLA Ops:
  125.5 2.0 %copy-start = (bf16[256,4096]{1,0:T(8,128)(2,1)S(1)}, bf16[256,4096]{1,0:T(8,128)(2,1)}, u32[]{:S(2)}) copy-start(bf16[256,4096]{1,0:T(8,128)(2,1)} %get-tuple-element.9) | copy-start | bytes 6291460
where the time goes:
time: 129 us
  Pallas kernels  125 us (97%)
  local copies, waits for them, and re-layouts  3.28 us (3%)
    pallas_call x1, Pallas kernels, local(): pl.pallas_call(functools.partial(kernel, dp, n, chunks), out_shape=(jax.S...  125 us
    unnamed x4, local copies, waits for them, and re-layouts  3.28 us

commit v1 on v0

v1 whole, which is shorter than its diff:
```python
import functools

import jax
import jax.numpy as jnp
from jax import lax
from jax.experimental import pallas as pl
from jax.experimental.pallas import tpu as pltpu
from jax.sharding import PartitionSpec as P

CHUNKS = 16
AHEAD = 2
AHEAD_Y = 12
CORES = 2
SIDE = 4
HOP = 1
PLANE = 1
MESH = pl.DeviceIdType.MESH


def grid_of(chips):
    fast = 1
    while (2 * fast) * (2 * fast) <= chips:
        fast *= 2
    return chips // fast, fast


def side_rows(tokens):
    return tokens * SIDE // 16


def kernel(dp, n, chunks, g_in, a_in, w_in, o_attn, o_w, gath, acts, acts_t, w, acc, part,
           z_send, z_recv, p_recv, ys_send, y_recv, f_recv, s_recv, a_send, a_recv, x_send, x_recv,
           own_sem, w_sem, own_a_sem):
    A, B = grid_of(n // CORES)
    tokens, width = g_in.shape
    heads = w_in.shape[0]
    F = width // chunks
    side = side_rows(tokens)
    line = A * tokens
    half = B * line
    me = lax.axis_index("context")
    rep = lax.axis_index("dp")
    c = lax.rem(me, CORES)
    b = lax.rem(me // CORES, B)
    a = me // (CORES * B)

    def ctx(a_, b_, c_):
        return (a_ * B + b_) * CORES + c_

    def others(i, size):
        return [lax.rem(i + d, size) for d in range(1, size)]

    def slot(i, t):
        s, bit = 0, 1
        while bit < A:
            s = s + bit * lax.rem(i // bit + t // bit, 2)
            bit *= 2
        return s

    pair = a + 1 - 2 * lax.rem(a, 2)

    def cols(k):
        return pl.ds(pl.multiple_of(k * F, F), F)

    def place(c_, u, s):
        return ((c_ * B + u) * A + s) * tokens

    def rows(k, lo, size):
        return gath.at[k, pl.ds(pl.multiple_of(lo, 16), size)]

    def own(k):
        return g_in.at[:, cols(k)]

    def remote(src, dst, send, recv, target):
        return pltpu.make_async_remote_copy(
            src_ref=src, dst_ref=dst, send_sem=send, recv_sem=recv, device_id=target, device_id_type=MESH)

    def inside(t):
        return jnp.logical_and(t >= 0, t < A)

    def own_copy(k):
        return pltpu.make_async_copy(own(k), rows(k, place(c, b, 0), tokens), own_sem.at[k])

    w_copy = pltpu.make_async_copy(w_in, w, w_sem)

    def head_cols(j):
        return pl.ds(pl.multiple_of(j * heads, heads), heads)

    own_act = pltpu.make_async_copy(a_in.at[:, head_cols(me)], acts.at[(c * B + b) * A], own_a_sem)

    own_act.start()
    w_copy.start()

    @pl.loop(0, chunks)
    def _(k):
        own_copy(k).start()

    barrier = pltpu.get_barrier_semaphore()
    for j in others(me, n):
        pl.semaphore_signal(barrier, inc=1, device_id={"context": j}, device_id_type=MESH)
    for r in others(rep, dp):
        pl.semaphore_signal(barrier, inc=1, device_id={"dp": r}, device_id_type=MESH)
    pl.semaphore_wait(barrier, n - 1 + dp - 1)

    def z_move(src, k, t, target):
        s = slot(target, t)
        return remote(src, rows(k, place(c, b, s), tokens), z_send.at[k], z_recv.at[k, s],
                      {"context": ctx(target, b, c)})

    def z_own(k):
        for sign in (1, -1):
            @pl.when(inside(a + sign))
            def _():
                z_move(own(k), k, a, a + sign).start()

    def y_own(k):
        for u in others(b, B):
            remote(own(k), rows(k, place(c, b, 0), tokens), ys_send.at[k], y_recv.at[k, b],
                   {"context": ctx(a, u, c)}).start()

    def side_moves(k):
        for u in others(b, B):
            got = rows(k, place(c, u, 0), tokens)
            remote(got, got, ys_send.at[k], y_recv.at[k, u], {"context": me}).wait_recv()
            remote(rows(k, place(c, u, 0), side), rows(k, place(c, u, 1), side), z_send.at[k], p_recv.at[k, u],
                   {"context": ctx(pair, b, c)}).start()

    def column_moves(k, d):
        for sign in (1, -1):
            t = a + sign * d

            @pl.when(inside(t))
            def _():
                s = slot(a, t)
                got = rows(k, place(c, b, s), tokens)
                remote(got, got, z_send.at[k], z_recv.at[k, s], {"context": me}).wait_recv()

                @pl.when(inside(a - sign))
                def _():
                    z_move(got, k, t, a - sign).start()

    def to_sibling(k, u):
        whole = rows(k, place(c, u, 0), line)
        remote(whole, whole, ys_send.at[k], s_recv.at[k], {"context": ctx(a, b, 1 - c)}).start()

    def rest(k, u):
        return rows(k, place(c, u, 1) + side, line - tokens - side)

    def line_moves(k):
        for u in others(b, B):
            remote(rest(k, b), rest(k, b), ys_send.at[k], f_recv.at[k, b], {"context": ctx(a, u, c)}).start()
        own_copy(k).wait()
        to_sibling(k, b)

    def plane_moves(k):
        for u in others(b, B):
            remote(rest(k, u), rest(k, u), ys_send.at[k], f_recv.at[k, u], {"context": me}).wait_recv()
            late = rows(k, place(c, u, 1), side)
            remote(late, late, z_send.at[k], p_recv.at[k, u], {"context": me}).wait_recv()
            to_sibling(k, u)

    def act_move(i, target):
        where = (c * B + b) * A + slot(target // (CORES * B), a)
        return remote(a_in.at[:, head_cols(target)], acts.at[where], a_send, a_recv, {"context": target})

    def x_moves(k):
        for r in others(rep, dp):
            remote(part.at[rep, k], part.at[rep, k], x_send.at[k], x_recv.at[k], {"dp": r}).start()

    for k in range(AHEAD):
        z_own(k)
    targets = others(me, n)
    for i, t in enumerate(targets):
        act_move(i, t).start()
    for k in range(AHEAD_Y):
        y_own(k)

    def compute(k):
        theirs = rows(k, place(1 - c, 0, 0), half)
        remote(theirs, theirs, ys_send.at[k], s_recv.at[k], {"context": me}).wait_recv()

        @pl.when(k == 0)
        def _():
            own_act.wait()
            w_copy.wait()
            most = acts.at[pl.ds(0, n - 1)]
            remote(most, most, a_send, a_recv, {"context": me}).wait_recv()
            for j in range(n):
                acts_t[:, j * tokens:(j + 1) * tokens] = acts[j].T
            acc[...] = jnp.zeros_like(acc)

        part[rep, k] = jnp.dot(acts_t[...], gath[k], preferred_element_type=jnp.float32).astype(part.dtype)
        x_moves(k)

        @pl.loop(0, CORES * B)
        def _(i):
            r = pl.ds(pl.multiple_of(i * line, line), line)
            total = acc[r] + lax.dot_general(
                gath[k, r], w[:, cols(k)], (((1,), (1,)), ((), ())), preferred_element_type=jnp.float32)

            @pl.when(k < chunks - 1)
            def _():
                acc[r] = total

            @pl.when(k == chunks - 1)
            def _():
                c_, u = i // B, lax.rem(i, B)
                for s in range(A):
                    to = ctx(slot(a, s), u, c_) * tokens
                    o_attn[pl.ds(pl.multiple_of(to, tokens), tokens)] = total[
                        s * tokens:(s + 1) * tokens].astype(o_attn.dtype)

    def finish(k):
        last = part.at[pl.ds(0, dp - 1), k]
        remote(last, last, x_send.at[k], x_recv.at[k], {"dp": rep}).wait_recv()
        total = part[0, k].astype(jnp.float32)
        for r in range(1, dp):
            total += part[r, k].astype(jnp.float32)
        o_w[:, cols(k)] = total.astype(o_w.dtype)

    def stage(k, f):
        pl.when(jnp.logical_and(k >= 0, k < chunks))(functools.partial(f, k))

    depth = HOP * (A - 2)

    @pl.loop(0, chunks + depth + PLANE + 2)
    def _(i):
        stage(i + AHEAD, z_own)
        stage(i + AHEAD_Y, y_own)
        for d in range(1, A):
            stage(i - HOP * (d - 1), lambda k, d=d: column_moves(k, d))
            if d == 1:
                stage(i, side_moves)
        stage(i - depth, line_moves)
        stage(i - depth - PLANE - 1, compute)
        stage(i - depth - PLANE, plane_moves)
        stage(i - depth - PLANE - 2, finish)

    edge = jnp.logical_or(a == 0, a == A - 1)

    def sent(ref, sem):
        remote(ref, ref, sem, s_recv.at[0], {"context": me}).wait_send()

    @pl.loop(0, chunks)
    def _(k):
        sent(rows(k, 0, half + (B - 1) * (line - side)), ys_send.at[k])
        sent(part.at[pl.ds(0, dp - 1), k], x_send.at[k])

        @pl.when(edge)
        def _():
            sent(rows(k, 0, tokens + (B - 1) * side), z_send.at[k])

        @pl.when(jnp.logical_not(edge))
        def _():
            sent(rows(k, 0, (A + 1) * tokens + (B - 1) * side), z_send.at[k])

    sent(acts.at[pl.ds(0, n - 1)], a_send)


def local(dp, n, grad_out, attn, w_out):
    g, x = grad_out[0], attn[0]
    tokens, width = g.shape
    heads = w_out.shape[0]
    length = tokens * n
    chunks = CHUNKS
    F = width // chunks
    A, B = grid_of(n // CORES)
    any_ = pl.BlockSpec(memory_space=pl.ANY)
    vmem = pl.BlockSpec(memory_space=pltpu.VMEM)
    bf = jnp.bfloat16
    dma = pltpu.SemaphoreType.DMA
    h, gw = pl.pallas_call(
        functools.partial(kernel, dp, n, chunks),
        out_shape=(jax.ShapeDtypeStruct((length, heads), bf), jax.ShapeDtypeStruct((heads, width), bf)),
        in_specs=[any_] * 3,
        out_specs=(vmem, vmem),
        scratch_shapes=[
            pltpu.VMEM((chunks, length, F), bf),
            pltpu.VMEM((n, tokens, heads), bf),
            pltpu.VMEM((heads, length), bf),
            pltpu.VMEM((heads, width), bf),
            pltpu.VMEM((length, heads), jnp.float32),
            pltpu.VMEM((dp, chunks, heads, F), bf),
            dma((chunks,)), dma((chunks, A)), dma((chunks, B)), dma((chunks,)), dma((chunks, B)), dma((chunks, B)),
            dma((chunks,)), dma, dma, dma((chunks,)), dma((chunks,)),
            dma((chunks,)), dma, dma,
        ],
        compiler_params=pltpu.CompilerParams(
            collective_id=0, has_side_effects=True, vmem_limit_bytes=52 * 2**20),
    )(g, x, w_out)
    return h[None], gw


def solution(mesh):
    dp, n = mesh.shape["dp"], mesh.shape["context"]
    in_specs = (P("dp", "context", None), P("dp", "context", None), P("context", None))
    out_specs = (P("dp", None, "context"), P("context", None))
    return jax.shard_map(functools.partial(local, dp, n), mesh=mesh, in_specs=in_specs, out_specs=out_specs,
                         check_vma=False)
```

time: 129 us -> 125 us (0.969)
  Pallas kernels: 125 us -> 121 us
    pallas_call x1, Pallas kernels: 125 us -> 121 us  [local(): pl.pallas_call(functools.partial(kernel, dp, n, chunks), out_shape=(jax.S...]
where the time goes in v1:
time: 125 us
  Pallas kernels  121 us (97%)
  local copies, waits for them, and re-layouts  3.28 us (3%)
    pallas_call x1, Pallas kernels, local(): pl.pallas_call(functools.partial(kernel, dp, n, chunks), out_shape=(jax.S...  121 us
    unnamed x4, local copies, waits for them, and re-layouts  3.28 us

profile of v1, /device:TPU:0, one launch (start us, length us, event | category | flops | bytes accessed | tf_op | source)
XLA Modules:
  0.0 124.6 jit_solution(10565338848141448568)
XLA Ops:
  0.6 120.7 %shard_map.50 = (bf16[2048,256]{1,0:T(8,128)(2,1)S(1)}, bf16[256,4096]{1,0:T(8,128)(2,1)}) custom-call(bf16[128,4096]{1,0:T(8,128)(2,1)} %bitcast.4, bf16[128,4096]{1,0:T(8,128)(2,1)} %bitcast.5, bf16[256,4096]{1,0:T(8,128)(2,1)} %w_in.1), custom_call_target="tpu_custom_call" | custom-call | tf_op jit(solution)/shard_map/pallas_call | solution.py:272
  121.3 0.0 copy-start
  121.3 1.0 copy.7
  122.3 1.0 copy-done
  123.3 1.3 %copy.8 = bf16[256,4096]{1,0:T(8,128)(2,1)} copy(bf16[256,4096]{1,0:T(8,128)(2,1)S(1)} %copy-done) | data formatting | bytes 4194304
Async XLA Ops:
  121.3 2.0 %copy-start = (bf16[256,4096]{1,0:T(8,128)(2,1)S(1)}, bf16[256,4096]{1,0:T(8,128)(2,1)}, u32[]{:S(2)}) copy-start(bf16[256,4096]{1,0:T(8,128)(2,1)} %get-tuple-element.9) | copy-start | bytes 6291460
